TPU v7x, 256 devices: a whole 4x4x8 slice. The times are simulated.
256 devices in a mesh: grp: 8 (over z), tp: 32 (over x, y, core).
Axes of the slice: x: 4, y: 4, z: 8, core: 2. Of those that a mesh axis runs over, the one named last changes fastest.
Arguments:
- hidden_in: bfloat16 [1024, 3584], P(('grp', 'tp')), may hold values from -6 to 6
- norm_gains: float32 [4, 3584], replicated, may hold values from 0.25 to 1.75
- w_qkv: bfloat16 [3584, 8192], P(None, 'tp'), may hold values from -0.09375 to 0.09375
- w_out: bfloat16 [4096, 3584], P('tp'), may hold values from -0.09375 to 0.09375
- w_gate_up: bfloat16 [2, 3584, 8192], P(None, None, 'tp'), may hold values from -0.09375 to 0.09375
- w_down: bfloat16 [8192, 3584], P('tp'), may hold values from -0.0625 to 0.0625
- prompt_keys: bfloat16 [32768, 2048], P(('grp', 'tp')), may hold values from -480 to 480, as said below
- prompt_values: bfloat16 [32768, 2048], P(('grp', 'tp')), may hold values from -6 to 6
- tail_keys: bfloat16 [1024, 64, 2048], P(('grp', 'tp')), may hold values from -480 to 480, as said below
- tail_values: bfloat16 [1024, 64, 2048], P(('grp', 'tp')), may hold values from -6 to 6
- prompt_len: int32 [80], replicated, may hold values from 1 to 4087, as said below
- group_home: int32 [80], replicated, may hold values from 0 to 7, as said below
- req_group: int32 [1024], P('grp'), may hold values from 0 to 79, as said below
- tail_len: int32 [1024], P('grp'), may hold values from 1 to 64, 32768 in all
Outputs:
- layer_out: bfloat16 [1024, 3584], P(('grp', 'tp'))
Inputs may be any that keep to these rules, and one draw needn't show every extreme that they name: `group_home`: each grp device is home to exactly 10 groups. `prompt_len`: the prompts of the groups homed on one grp device lie one after another in order of group id from the first of that device's 4096 cache positions; together they hold at most 4096 positions, exactly 4096 on one home in every draw, where one group holds 4087 of them. `req_group`: of the 128 requests held by one grp device, at most 32 belong to groups homed on any one grp device; in every draw one home receives exactly 32 requests from every grp device. `prompt_keys`: cached keys, already rotated. `tail_keys`: cached keys, already rotated.
All inputs are finite; a program needn't handle non-finite values. No bound on the sum of `tail_len` on one device may be relied on, other than what follows from the above.
Results may differ from a plain program's by a relative error of at most 0.015.
Values may be sent and summed in bfloat16 or wider, within the bound.
A program may use at most 128 MiB of HBM per device.

v0:
```python
import math
import jax
import jax.numpy as jnp
from jax import lax
from jax.sharding import PartitionSpec as P

HEADS = 16
KV_HEADS = 8
HEAD_DIM = 256
NORM_EPS = 1e-06
SOFT_CAP = 50.0


def rms_scale(values, gain_row):
    values = values.astype(jnp.float32)
    return (
        values * lax.rsqrt(jnp.mean(values * values, axis=-1, keepdims=True) + NORM_EPS) * gain_row
    )


def rotate(head_rows, position):
    half_width = head_rows.shape[-1] // 2
    freq_index = jnp.arange(half_width).astype(jnp.float32)
    frequency = jnp.exp(freq_index * (-math.log(10000.0) / half_width))
    angles = position.astype(jnp.float32)[:, None] * frequency[None, :]
    cosine = jnp.cos(angles)[:, None, :]
    sine_part = jnp.sin(angles)[:, None, :]
    head_rows = head_rows.astype(jnp.float32)
    first_half = head_rows[..., :half_width]
    second = head_rows[..., half_width:]
    return jnp.concatenate(
        [first_half * cosine - second * sine_part, second * cosine + first_half * sine_part],
        axis=-1,
    )


def capped(scores):
    return SOFT_CAP * jnp.tanh(scores * HEAD_DIM ** (-0.5) / SOFT_CAP)


def lookup(lookup_table, index_list):
    matches = index_list[:, None] == jnp.arange(lookup_table.shape[0], dtype=jnp.int32)[None, :]
    return jnp.sum(jnp.where(matches, lookup_table[None, :], 0), axis=1)


def group_starts(prompt_len, group_home):
    group_ids = jnp.arange(prompt_len.shape[0], dtype=jnp.int32)
    same_home = group_home[:, None] == group_home[None, :]
    earlier = group_ids[None, :] < group_ids[:, None]
    return jnp.sum(jnp.where(same_home & earlier, prompt_len[None, :], 0), axis=1)


def shared_part(queries, key_rows, value_rows, visible):
    scores = capped(
        jnp.einsum("nkjd,pkd->nkjp", queries, key_rows, preferred_element_type=jnp.float32)
    )
    exponent = jnp.where(visible[:, None, None, :], jnp.exp(scores), 0.0)
    numerator = jnp.einsum(
        "nkjp,pkd->nkjd",
        exponent.astype(jnp.bfloat16),
        value_rows,
        preferred_element_type=jnp.float32,
    )
    return (numerator, jnp.sum(exponent, axis=-1))


def own_part(queries, key_rows, value_rows, visible):
    scores = capped(
        jnp.einsum("nkjd,npkd->nkjp", queries, key_rows, preferred_element_type=jnp.float32)
    )
    exponent = jnp.where(visible[:, None, None, :], jnp.exp(scores), 0.0)
    numerator = jnp.einsum(
        "nkjp,npkd->nkjd",
        exponent.astype(jnp.bfloat16),
        value_rows,
        preferred_element_type=jnp.float32,
    )
    return (numerator, jnp.sum(exponent, axis=-1))


def per_device(
    hidden_in,
    norm_gains,
    w_qkv,
    w_out,
    w_gate_up,
    w_down,
    prompt_keys,
    prompt_values,
    tail_keys,
    tail_values,
    prompt_len,
    group_home,
    req_group,
    tail_len,
):
    tp_rank = lax.axis_index("tp")
    q_width = HEADS * HEAD_DIM
    kv_width = KV_HEADS * HEAD_DIM
    row_count = hidden_in.shape[0]
    normed = rms_scale(hidden_in, norm_gains[0]).astype(jnp.bfloat16)
    qkv_share = jnp.dot(
        lax.all_gather(normed, "tp", axis=0, tiled=True), w_qkv, preferred_element_type=jnp.float32
    ).astype(jnp.bfloat16)
    projected_qkv = lax.all_gather(qkv_share, "tp", axis=1, tiled=True)
    requests = projected_qkv.shape[0]
    req_len = lookup(prompt_len, req_group)
    position = req_len + tail_len
    queries = rotate(
        projected_qkv[:, :q_width].reshape(requests, HEADS, HEAD_DIM), position
    ).astype(jnp.bfloat16)
    queries = queries.reshape(requests, KV_HEADS, 2, HEAD_DIM)
    key_new = rotate(
        projected_qkv[:, q_width : q_width + kv_width].reshape(requests, KV_HEADS, HEAD_DIM),
        position,
    ).astype(jnp.bfloat16)
    value_new = projected_qkv[:, q_width + kv_width :].reshape(requests, KV_HEADS, HEAD_DIM)
    starts = group_starts(prompt_len, group_home)
    req_home = lookup(group_home, req_group)
    req_start = lookup(starts, req_group)
    cap_dev = prompt_keys.shape[0]
    row_first = tp_rank * row_count
    own_queries = lax.dynamic_slice_in_dim(queries, row_first, row_count, 0)
    own_tail_len = lax.dynamic_slice_in_dim(tail_len, row_first, row_count, 0)
    tail_dev = tail_keys.shape[1]
    tail_pos = jnp.arange(tail_dev, dtype=jnp.int32)
    own_num, own_den = own_part(
        own_queries,
        tail_keys.reshape(row_count, tail_dev, KV_HEADS, HEAD_DIM),
        tail_values.reshape(row_count, tail_dev, KV_HEADS, HEAD_DIM),
        tail_pos[None, :] < own_tail_len[:, None],
    )
    numerator = lax.dynamic_update_slice_in_dim(
        jnp.zeros((requests, KV_HEADS, 2, HEAD_DIM), jnp.float32), own_num, row_first, 0
    )
    denominator = lax.dynamic_update_slice_in_dim(
        jnp.zeros((requests, KV_HEADS, 2), jnp.float32), own_den, row_first, 0
    )
    key_piece = lax.all_gather(prompt_keys, "grp", axis=0, tiled=True)
    value_piece = lax.all_gather(prompt_values, "grp", axis=0, tiled=True)
    piece_rows = key_piece.shape[0]
    gathered_index = jnp.arange(piece_rows, dtype=jnp.int32)
    home_index = gathered_index // cap_dev
    piece_offsets = tp_rank * cap_dev + gathered_index % cap_dev
    visible = (
        (home_index[None, :] == req_home[:, None])
        & (piece_offsets[None, :] >= req_start[:, None])
        & (piece_offsets[None, :] < (req_start + req_len)[:, None])
    )
    part_num, part_den = shared_part(
        queries,
        key_piece.reshape(piece_rows, KV_HEADS, HEAD_DIM),
        value_piece.reshape(piece_rows, KV_HEADS, HEAD_DIM),
        visible,
    )
    numerator, denominator = (numerator + part_num, denominator + part_den)
    share_width = w_out.shape[0]
    first_col = tp_rank * share_width
    flat_num = numerator.reshape(requests, q_width)
    flat_den = denominator.reshape(requests, HEADS)
    total_num, total_den = lax.psum((flat_num, flat_den), "tp")
    share_num = lax.dynamic_slice_in_dim(total_num, first_col, share_width, 1)
    self_exp = jnp.exp(
        capped(jnp.einsum("nkjd,nkd->nkj", queries, key_new, preferred_element_type=jnp.float32))
    )
    self_num = (
        lax.optimization_barrier(self_exp.astype(jnp.bfloat16)).astype(jnp.float32)[..., None]
        * value_new.astype(jnp.float32)[:, :, None, :]
    )
    self_share = lax.dynamic_slice_in_dim(
        self_num.reshape(requests, q_width), first_col, share_width, 1
    )
    total_den = total_den + self_exp.reshape(requests, HEADS)
    head_of_col = (first_col + jnp.arange(share_width, dtype=jnp.int32)) // HEAD_DIM
    head_pick = (head_of_col[None, :] == jnp.arange(HEADS, dtype=jnp.int32)[:, None]).astype(
        jnp.float32
    )
    den_cols = jnp.dot(total_den, head_pick, precision=lax.Precision.HIGHEST)
    attn_share = ((share_num + self_share) / den_cols).astype(jnp.bfloat16)
    block_rows = attn_share
    attn_proj = lax.psum_scatter(
        jnp.dot(block_rows, w_out, preferred_element_type=jnp.float32),
        "tp",
        scatter_dimension=0,
        tiled=True,
    )
    resid = (hidden_in.astype(jnp.float32) + rms_scale(attn_proj, norm_gains[1])).astype(
        jnp.bfloat16
    )
    ffn_in = rms_scale(resid, norm_gains[2]).astype(jnp.bfloat16)
    gate_up = jnp.einsum(
        "rd,kdf->krf",
        lax.all_gather(ffn_in, "tp", axis=0, tiled=True),
        w_gate_up,
        preferred_element_type=jnp.float32,
    )
    hidden_units = (jax.nn.gelu(gate_up[0], approximate=True) * gate_up[1]).astype(jnp.bfloat16)
    block_rows = hidden_units
    ffn_proj = lax.psum_scatter(
        jnp.dot(block_rows, w_down, preferred_element_type=jnp.float32).astype(jnp.bfloat16),
        "tp",
        scatter_dimension=0,
        tiled=True,
    ).astype(jnp.float32)
    return (resid.astype(jnp.float32) + rms_scale(ffn_proj, norm_gains[3])).astype(jnp.bfloat16)


def solution(mesh):
    in_specs = (
        P(("grp", "tp"), None),
        P(),
        P(None, "tp"),
        P("tp", None),
        P(None, None, "tp"),
        P("tp", None),
        P(("grp", "tp"), None),
        P(("grp", "tp"), None),
        P(("grp", "tp"), None, None),
        P(("grp", "tp"), None, None),
        P(),
        P(),
        P("grp"),
        P("grp"),
    )
    out_specs = P(("grp", "tp"), None)
    return jax.shard_map(
        per_device, mesh=mesh, in_specs=in_specs, out_specs=out_specs, check_vma=False
    )
```

profile of v0, /device:TPU:1, one launch (start us, length us, event | category | flops | bytes accessed | tf_op | source)
XLA Modules:
  0.0 625.6 jit_solution(4266515688802575155)
XLA Ops:
  9.5 26.6 %all-gather = bf16[32,4,3584]{2,1,0:T(4,128)(2,1)S(1)} all-gather(bf16[1,4,3584]{2,1,0:T(4,128)(2,1)S(1)} %fusion.47), channel_id=1, replica_groups=mesh['grp'=8,'tp'=32] {'tp'}, dimensions={0}, use_global_device_ids=true | all-gather | bytes 946176 | tf_op jit(solution)/shard_map/all_gather | solution.py:103
  37.2 2.9 convolution_convert_fusion.1
  44.0 46.5 %all-gather.6.cloned.1.call-done = bf16[128,8192]{1,0:T(8,128)(2,1)} async-done(((bf16[128,256]{1,0:T(8,128)(2,1)}), bf16[128,8192]{1,0:T(8,128)(2,1)}) %all-gather.6.cloned.1.call-update) | async-done | bytes 2097168 | tf_op jit(solution)/shard_map/all_gather | solution.py:105
  90.5 1.4 slice_convert_fusion
  94.7 2.4 slice_convert_fusion.2
  99.2 50.9 %all-gather.8.cloned.1.call-done = bf16[1024,2048]{0,1:T(8,128)(2,1)} async-done(((bf16[128,2048]{0,1:T(8,128)(2,1)}), bf16[1024,2048]{0,1:T(8,128)(2,1)}) %all-gather.8.cloned.1.call-update) | async-done | bytes 4194320 | tf_op jit(solution)/shard_map/all_gather | solution.py:139
  150.1 7.7 %bitcast_reduce_fusion = (f32[128,8,2]{0,2,1:T(2,128)S(1)}, f32[8,128,2,1024]{3,1,2,0:T(8,128)}) fusion(pred[128,1024]{1,0:T(8,128)(4,1)} %compare_and_fusion, bf16[1024,8,256,1]{0,2,3,1:T(8,128)(2,1)} %bitcast.96, bf16[128,8,2,128]{3,0,2,1:T(8,128)(2,1)S(1)} %bitcast.87, bf16[128,8,2,128]{3,0,2,1:T(8,128)(2,1)S(1)} %bitcast.84), kind=kOutput, calls=%fused_computation | convolution fusion | flops 1084225536 | bytes 13770752 | tf_op jit(solution)/shard_map/nkjd,pkd->nkjp/dot_general | solution.py:55
  157.8 55.1 %all-gather.10.cloned.1.call-done = bf16[1024,2048]{0,1:T(8,128)(2,1)} async-done(((bf16[128,2048]{0,1:T(8,128)(2,1)}), bf16[1024,2048]{0,1:T(8,128)(2,1)}) %all-gather.10.cloned.1.call-update) | async-done | bytes 4194320 | tf_op jit(solution)/shard_map/all_gather | solution.py:140
  212.9 7.0 %fusion = f32[8,128,2,256]{3,1,2,0:T(8,128)S(1)} fusion(bf16[1024,8,256,1]{0,2,3,1:T(8,128)(2,1)} %bitcast.97, f32[8,128,2,1024]{3,1,2,0:T(8,128)} %get-tuple-element.27, pred[128,1024]{1,0:T(8,128)(4,1)} %compare_and_fusion), kind=kOutput, calls=%fused_computation.4 | convolution fusion | flops 1082130432 | bytes 14811136 | tf_op jit(solution)/shard_map/nkjp,pkd->nkjd/dot_general | solution.py:58
  222.0 2.9 copy.85
  224.9 2.9 copy.86
  228.1 3.4 fusion.15
  233.3 2.8 broadcast_multiply_fusion
  236.1 4.0 mul.269
  241.4 67.5 %psum.15 = f32[128,16]{0,1:T(8,128)S(1)} all-reduce(f32[128,16]{0,1:T(8,128)S(1)} %bitcast.94), channel_id=1, replica_groups=mesh['grp'=8,'tp'=32] {'tp'}, use_global_device_ids=true, to_apply=%region_8.9 | all-reduce | flops 2048 | bytes 16384 | tf_op jit(solution)/shard_map/psum | solution.py:161
  309.0 38.9 %all-reduce.6.cloned.1.call-done = f32[128,4096]{1,0:T(8,128)} async-done(((f32[128,4096]{1,0:T(8,128)}), f32[128,4096]{1,0:T(8,128)}) %all-reduce.6.cloned.1.call-update) | async-done | bytes 2097168 | tf_op jit(solution)/shard_map/psum | solution.py:161
  349.1 1.6 fusion.74
  352.0 115.3 %all-reduce.8.cloned.1.call-done = f32[128,3584]{1,0:T(8,128)} async-done(((f32[128,3584]{1,0:T(8,128)}), f32[128,3584]{1,0:T(8,128)}) %all-reduce.8.cloned.1.call-update) | async-done | bytes 1835024
  469.6 28.2 %all-gather.1 = bf16[32,4,3584]{2,1,0:T(4,128)(2,1)} all-gather(bf16[1,4,3584]{2,1,0:T(4,128)(2,1)S(1)} %fusion.46), channel_id=1, replica_groups=mesh['grp'=8,'tp'=32] {'tp'}, dimensions={0}, use_global_device_ids=true | all-gather | bytes 946176 | tf_op jit(solution)/shard_map/all_gather | solution.py:193
  497.9 1.7 reshape.286
  499.5 2.7 convolution_bitcast_fusion
  502.2 1.4 convolution_convert_fusion
  503.7 112.7 %all-reduce.10.cloned.1.call-done = bf16[128,3584]{1,0:T(8,128)(2,1)} async-done(((bf16[128,3584]{1,0:T(8,128)(2,1)}), bf16[128,3584]{1,0:T(8,128)(2,1)}) %all-reduce.10.cloned.1.call-update) | async-done | bytes 917520
  617.3 1.5 fusion.42
  (85 shorter events, 23.2 us)
Async XLA Ops:
  6.5 495.7 %copy-start = (bf16[256,3584]{1,0:T(8,128)(2,1)S(1)}, bf16[256,3584]{1,0:T(8,128)(2,1)}, u32[]{:S(2)}) copy-start(bf16[256,3584]{1,0:T(8,128)(2,1)} %param.19) | copy-start | bytes 5505028
  6.5 83.9 %all-gather.6.cloned.1.call-start = ((), (), s32[]{:S(2)}) async-start(), calls=%async_computation | async-start | bytes 2162688 | tf_op jit(solution)/shard_map/all_gather | solution.py:105
  36.0 4.1 copy-start.4
  37.2 4.0 copy-start.5
  40.0 2.3 copy-start.10
  40.1 2.4 copy-start.7
  40.1 2.4 copy-start.8
  40.1 2.6 copy-start.9
  40.1 110.0 %all-gather.8.cloned.1.call-start = ((), (), s32[]{:S(2)}) async-start(), calls=%async_computation.1 | async-start | bytes 4718592 | tf_op jit(solution)/shard_map/all_gather | solution.py:139
  41.2 171.8 %all-gather.10.cloned.1.call-start = ((), (), s32[]{:S(2)}) async-start(), calls=%async_computation.2 | async-start | bytes 4718592 | tf_op jit(solution)/shard_map/all_gather | solution.py:140
  42.3 305.7 %all-reduce.6.cloned.1.call-start = ((), (), s32[]{:S(2)}) async-start(), calls=%async_computation.3 | async-start | bytes 4194304 | tf_op jit(solution)/shard_map/psum | solution.py:161
  92.9 1.2 copy-start.11
  97.5 1.4 copy-start.2
  227.8 5.1 copy-start.1
  227.8 239.5 %all-reduce.8.cloned.1.call-start = ((), (), s32[]{:S(2)}) async-start(), calls=%async_computation.4 | async-start | bytes 3670016
  236.1 113.0 %copy-start.3 = (bf16[128,3584]{1,0:T(8,128)(2,1)S(1)}, bf16[128,3584]{1,0:T(8,128)(2,1)}, u32[]{:S(2)}) copy-start(bf16[128,3584]{1,0:T(8,128)(2,1)} %param.17) | copy-start | bytes 2752516
  349.1 1.7 copy-start.12
  349.1 119.3 %copy-start.6 = (bf16[4,3584]{1,0:T(4,128)(2,1)S(1)}, bf16[4,3584]{1,0:T(4,128)(2,1)}, u32[]{:S(2)}) copy-start(bf16[4,3584]{1,0:T(4,128)(2,1)} %param.14) | copy-start | bytes 86020
  350.7 265.6 %all-reduce.10.cloned.1.call-start = ((), (), s32[]{:S(2)}) async-start(), calls=%async_computation.5 | async-start | bytes 1835008
Sparse Core Ops, SparseCore 0:
  40.2 50.2 all-gather.5
  92.2 57.8 all-gather.7
  151.8 61.1 all-gather.9
  228.0 119.9 all-reduce.5
  351.1 116.2 all-reduce.7
  503.8 112.4 all-reduce.9
where the time goes:
time: 626 us
  waiting for transfers between devices  419 us (67%)
  blocking collectives  122 us (19%)
  matrix products  28.5 us (5%)
  local copies, waits for them, and re-layouts  23.3 us (4%)
  other arithmetic  17.2 us (3%)
  between operations  14.4 us (2%)
    unnamed x8, waiting for transfers between devices  228 us
    psum x1, blocking collectives, per_device(): total_num, total_den = lax.psum((flat_num, flat_den), 'tp')  67.5 us
    all_gather x1, waiting for transfers between devices, per_device(): value_piece = lax.all_gather(prompt_values, 'grp', axis=0, tiled=True)  55.1 us
    all_gather x1, waiting for transfers between devices, per_device(): key_piece = lax.all_gather(prompt_keys, 'grp', axis=0, tiled=True)  50.9 us
    all_gather x1, waiting for transfers between devices, per_device(): projected_qkv = lax.all_gather(qkv_share, 'tp', axis=1, tiled=True)  46.5 us
    psum x1, waiting for transfers between devices, per_device(): total_num, total_den = lax.psum((flat_num, flat_den), 'tp')  38.9 us
    all_gather x1, blocking collectives, per_device(): lax.all_gather(ffn_in, 'tp', axis=0, tiled=True)  28.2 us
    all_gather x1, blocking collectives, per_device(): lax.all_gather(normed, 'tp', axis=0, tiled=True)  26.6 us
  transfers between devices with their start and end apart: 6, of which 6 were waited for; matrix products, arithmetic and copies ran while one was open for 5% of the time, Pallas kernels for 0%

commit v1 on v0

--- a/solution.py
+++ b/solution.py
@@ -137,7 +137,22 @@
         jnp.zeros((requests, KV_HEADS, 2), jnp.float32), own_den, row_first, 0
     )
     key_piece = lax.all_gather(prompt_keys, "grp", axis=0, tiled=True)
-    value_piece = lax.all_gather(prompt_values, "grp", axis=0, tiled=True)
+    ways, here, step = (lax.axis_size("grp"), lax.axis_index("grp"), prompt_values.shape[0])
+    shape = [n * ways if d == 0 else n for d, n in enumerate(prompt_values.shape)]
+    value_piece = lax.dynamic_update_slice_in_dim(
+        jnp.zeros(shape, prompt_values.dtype), prompt_values, here * step, axis=0
+    )
+    going_up = going_down = prompt_values
+    for far in range(1, ways // 2 + 1):
+        going_up = lax.ppermute(going_up, "grp", [(d, (d + 1) % ways) for d in range(ways)])
+        value_piece = lax.dynamic_update_slice_in_dim(
+            value_piece, going_up, (here - far) % ways * step, axis=0
+        )
+        if 2 * far < ways:
+            going_down = lax.ppermute(going_down, "grp", [(d, (d - 1) % ways) for d in range(ways)])
+            value_piece = lax.dynamic_update_slice_in_dim(
+                value_piece, going_down, (here + far) % ways * step, axis=0
+            )
     piece_rows = key_piece.shape[0]
     gathered_index = jnp.arange(piece_rows, dtype=jnp.int32)
     home_index = gathered_index // cap_dev

time: 626 us -> 577 us (0.922)
  waiting for transfers between devices: 419 us -> 330 us
  local copies, waits for them, and re-layouts: 23.3 us -> 52.2 us
  starting transfers between devices: 0.39 us -> 11.3 us
    all_gather x1 -> x0, waiting for transfers between devices: 55.1 us -> none  [per_device(): value_piece = lax.all_gather(prompt_values, 'grp', axis=0, tiled=True)]
    all_gather x1, waiting for transfers between devices: 46.5 us -> 0.01 us  [per_device(): projected_qkv = lax.all_gather(qkv_share, 'tp', axis=1, tiled=True)]
    ppermute x0 -> x7, waiting for transfers between devices: none -> 26.1 us  [the longest x4 26.1 us: per_device(): lax.ppermute(going_up, 'grp', [(d, (d + 1) % ways) for d in range(ways)])]
    all_gather x1, waiting for transfers between devices: 50.9 us -> 36.6 us  [per_device(): key_piece = lax.all_gather(prompt_keys, 'grp', axis=0, tiled=True)]
    ppermute x0 -> x7, starting transfers between devices: none -> 11.2 us  [the longest x3 9.46 us: per_device(): lax.ppermute(going_down, 'grp', [(d, (d - 1) % ways) for d in range(ways)])]
    add x2, local copies, waits for them, and re-layouts: 4.17 us -> 13.6 us  [per_device(): numerator, denominator = (numerator + part_num, denominator + part_den)]
    dynamic_update_slice x0 -> x8, local copies, waits for them, and re-layouts: none -> 7.12 us  [the longest x4 3.53 us: per_device(): lax.dynamic_update_slice_in_dim(value_piece, going_up, (here - far) % way...]
    unnamed x8 -> x7, waiting for transfers between devices: 228 us -> 228 us
  transfers between devices with their start and end apart: 6 -> 12, of which waited for: 6 -> 8; matrix products, arithmetic and copies ran while one was open for 5% -> 8% of each run, Pallas kernels for 0% -> 0%
where the time goes in v1:
time: 577 us; the launch traced here: 576 us
  waiting for transfers between devices  330 us (57%)
  blocking collectives  122 us (21%)
  local copies, waits for them, and re-layouts  52.2 us (9%)
  matrix products  24.6 us (4%)
  other arithmetic  20.6 us (4%)
  between operations  14.3 us (2%)
  starting transfers between devices  11.3 us (2%)
    unnamed x7, waiting for transfers between devices  228 us
    psum x1, blocking collectives, per_device(): total_num, total_den = lax.psum((flat_num, flat_den), 'tp')  67.7 us
    psum x1, waiting for transfers between devices, per_device(): total_num, total_den = lax.psum((flat_num, flat_den), 'tp')  39.2 us
    all_gather x1, waiting for transfers between devices, per_device(): key_piece = lax.all_gather(prompt_keys, 'grp', axis=0, tiled=True)  36.6 us
    all_gather x1, blocking collectives, per_device(): lax.all_gather(ffn_in, 'tp', axis=0, tiled=True)  28.2 us
    all_gather x1, blocking collectives, per_device(): lax.all_gather(normed, 'tp', axis=0, tiled=True)  26.6 us
    ppermute x4, waiting for transfers between devices, per_device(): lax.ppermute(going_up, 'grp', [(d, (d + 1) % ways) for d in range(ways)])  26.1 us
    add x2, local copies, waits for them, and re-layouts, per_device(): numerator, denominator = (numerator + part_num, denominator + part_den)  13.6 us
  transfers between devices with their start and end apart: 12, of which 8 were waited for; matrix products, arithmetic and copies ran while one was open for 8% of the time, Pallas kernels for 0%

profile of v1, /device:TPU:1, one launch (start us, length us, event | category | flops | bytes accessed | tf_op | source)
XLA Modules:
  0.0 575.6 jit_solution(2298308670800013352)
XLA Ops:
  10.1 26.6 %all-gather = bf16[32,4,3584]{2,1,0:T(4,128)(2,1)S(1)} all-gather(bf16[1,4,3584]{2,1,0:T(4,128)(2,1)S(1)} %fusion.46), channel_id=1, replica_groups=mesh['grp'=8,'tp'=32] {'tp'}, dimensions={0}, use_global_device_ids=true | all-gather | bytes 946176 | tf_op jit(solution)/shard_map/all_gather | solution.py:103
  37.8 2.9 convolution_convert_fusion.1
  43.6 4.0 collective-permute-start.1
  51.9 7.7 %collective-permute-done = bf16[128,2048]{1,0:T(8,128)(2,1)S(1)} collective-permute-done((bf16[128,2048]{1,0:T(8,128)(2,1)S(1)}, bf16[128,2048]{1,0:T(8,128)(2,1)S(1)}, u32[]{:S(2)}, u32[]{:S(2)}) %collective-permute-start) | collective-permute-done | bytes 524320 | tf_op jit(solution)/shard_map/ppermute | solution.py:147
  60.3 2.7 collective-permute-start.3
  64.9 2.5 broadcast_in_dim.58
  68.6 5.1 collective-permute-done.2
  74.9 2.8 collective-permute-start.5
  82.1 5.1 collective-permute-done.4
  91.4 8.2 %collective-permute-done.6 = bf16[128,2048]{1,0:T(8,128)(2,1)} collective-permute-done((bf16[128,2048]{1,0:T(8,128)(2,1)S(1)}, bf16[128,2048]{1,0:T(8,128)(2,1)}, u32[]{:S(2)}, u32[]{:S(2)}) %collective-permute-start.6) | collective-permute-done | bytes 524320 | tf_op jit(solution)/shard_map/ppermute | solution.py:147
  114.0 36.6 %all-gather.7.cloned.1.call-done = bf16[1024,2048]{0,1:T(8,128)(2,1)} async-done(((bf16[128,2048]{0,1:T(8,128)(2,1)}), bf16[1024,2048]{0,1:T(8,128)(2,1)}) %all-gather.7.cloned.1.call-update) | async-done | bytes 4194320 | tf_op jit(solution)/shard_map/all_gather | solution.py:139
  150.7 5.4 bitcast_reduce_fusion
  156.1 4.8 fusion
  162.8 12.3 %add.220 = f32[128,8,2,256]{0,3,2,1:T(8,128)} dynamic-update-slice(f32[128,8,2,256]{0,3,2,1:T(8,128)} %bitcast.77, f32[4,8,2,256]{0,3,2,1:T(8,128)} %bitcast_add_fusion, s32[]{:T(128)S(6)} %select_n.137, s32[]{:T(128)} %constant.118.clone.1, s32[]{:T(128)} %constant.118.clone.1, s32[]{:T(128)} %constant.118.clone.1) | dynamic-update-slice | bytes 131076 | tf_op jit(solution)/shard_map/add | solution.py:171
  175.1 2.9 copy.137
  178.1 3.4 fusion.15
  183.0 2.8 broadcast_multiply_fusion
  185.8 4.0 mul.301
  191.3 67.7 %psum.15 = f32[128,16]{0,1:T(8,128)S(1)} all-reduce(f32[128,16]{0,1:T(8,128)S(1)} %bitcast.92), channel_id=1, replica_groups=mesh['grp'=8,'tp'=32] {'tp'}, use_global_device_ids=true, to_apply=%region_8.9 | all-reduce | flops 2048 | bytes 16384 | tf_op jit(solution)/shard_map/psum | solution.py:176
  259.0 39.2 %all-reduce.6.cloned.1.call-done = f32[128,4096]{1,0:T(8,128)} async-done(((f32[128,4096]{1,0:T(8,128)}), f32[128,4096]{1,0:T(8,128)}) %all-reduce.6.cloned.1.call-update) | async-done | bytes 2097168 | tf_op jit(solution)/shard_map/psum | solution.py:176
  302.2 115.4 %all-reduce.8.cloned.1.call-done = f32[128,3584]{1,0:T(8,128)} async-done(((f32[128,3584]{1,0:T(8,128)}), f32[128,3584]{1,0:T(8,128)}) %all-reduce.8.cloned.1.call-update) | async-done | bytes 1835024
  419.9 28.2 %all-gather.1 = bf16[32,4,3584]{2,1,0:T(4,128)(2,1)} all-gather(bf16[1,4,3584]{2,1,0:T(4,128)(2,1)S(1)} %fusion.45), channel_id=1, replica_groups=mesh['grp'=8,'tp'=32] {'tp'}, dimensions={0}, use_global_device_ids=true | all-gather | bytes 946176 | tf_op jit(solution)/shard_map/all_gather | solution.py:208
  449.8 2.7 convolution_bitcast_fusion
  453.9 112.7 %all-reduce.10.cloned.1.call-done = bf16[128,3584]{1,0:T(8,128)(2,1)} async-done(((bf16[128,3584]{1,0:T(8,128)(2,1)}), bf16[128,3584]{1,0:T(8,128)(2,1)}) %all-reduce.10.cloned.1.call-update) | async-done | bytes 917520
  (124 shorter events, 55.9 us)
Async XLA Ops:
  6.5 445.9 %copy-start = (bf16[256,3584]{1,0:T(8,128)(2,1)S(1)}, bf16[256,3584]{1,0:T(8,128)(2,1)}, u32[]{:S(2)}) copy-start(bf16[256,3584]{1,0:T(8,128)(2,1)} %param.19) | copy-start | bytes 5505028
  6.5 34.2 %copy-start.7 = (bf16[128,2048]{1,0:T(8,128)(2,1)S(1)}, bf16[128,2048]{1,0:T(8,128)(2,1)}, u32[]{:S(2)}) copy-start(bf16[128,2048]{1,0:T(8,128)(2,1)} %param.20) | copy-start | bytes 1572868
  6.5 95.2 %all-gather.5.cloned.1.call-start = ((), (), s32[]{:S(2)}) async-start(), calls=%async_computation | async-start | bytes 2162688 | tf_op jit(solution)/shard_map/all_gather | solution.py:105
  40.7 110.0 %all-gather.7.cloned.1.call-start = ((), (), s32[]{:S(2)}) async-start(), calls=%async_computation.1 | async-start | bytes 4718592 | tf_op jit(solution)/shard_map/all_gather | solution.py:139
  41.8 256.3 %all-reduce.6.cloned.1.call-start = ((), (), s32[]{:S(2)}) async-start(), calls=%async_computation.2 | async-start | bytes 4194304 | tf_op jit(solution)/shard_map/psum | solution.py:176
  41.9 17.8 %collective-permute-start = (bf16[128,2048]{1,0:T(8,128)(2,1)S(1)}, bf16[128,2048]{1,0:T(8,128)(2,1)S(1)}, u32[]{:S(2)}, u32[]{:S(2)}) collective-permute-start(bf16[128,2048]{1,0:T(8,128)(2,1)S(1)} %copy-done.8), channel_id=1, source_target_pairs={{0,32},{32,64},{64,96},{96,128},{128,160},{160,192},{192,224},{224... | collective-permute-start | bytes 1572872 | tf_op jit(solution)/shard_map/ppermute | solution.py:147
  43.6 16.7 %collective-permute-start.1 = (bf16[128,2048]{1,0:T(8,128)(2,1)S(1)}, bf16[128,2048]{1,0:T(8,128)(2,1)S(1)}, u32[]{:S(2)}, u32[]{:S(2)}) collective-permute-start(bf16[128,2048]{1,0:T(8,128)(2,1)S(1)} %copy-done.8), channel_id=1, source_target_pairs={{0,224},{32,0},{64,32},{96,64},{128,96},{160,128},{192,160},{224,1... | collective-permute-start | bytes 1572872 | tf_op jit(solution)/shard_map/ppermute | solution.py:152
  59.7 14.1 %collective-permute-start.2 = (bf16[128,2048]{1,0:T(8,128)(2,1)S(1)}, bf16[128,2048]{1,0:T(8,128)(2,1)}, u32[]{:S(2)}, u32[]{:S(2)}) collective-permute-start(bf16[128,2048]{1,0:T(8,128)(2,1)S(1)} %collective-permute-done), channel_id=1, source_target_pairs={{0,32},{32,64},{64,96},{96,128},{128,160},{160,192},{192,224},{224... | collective-permute-start | bytes 1572872 | tf_op jit(solution)/shard_map/ppermute | solution.py:147
  60.3 14.6 %collective-permute-start.3 = (bf16[128,2048]{1,0:T(8,128)(2,1)S(1)}, bf16[128,2048]{1,0:T(8,128)(2,1)}, u32[]{:S(2)}, u32[]{:S(2)}) collective-permute-start(bf16[128,2048]{1,0:T(8,128)(2,1)S(1)} %collective-permute-done.1), channel_id=1, source_target_pairs={{0,224},{32,0},{64,32},{96,64},{128,96},{160,128},{192,160},{224,1... | collective-permute-start | bytes 1572872 | tf_op jit(solution)/shard_map/ppermute | solution.py:152
  73.7 13.4 %collective-permute-start.4 = (bf16[128,2048]{1,0:T(8,128)(2,1)}, bf16[128,2048]{1,0:T(8,128)(2,1)S(1)}, u32[]{:S(2)}, u32[]{:S(2)}) collective-permute-start(bf16[128,2048]{1,0:T(8,128)(2,1)} %collective-permute-done.2), channel_id=1, source_target_pairs={{0,32},{32,64},{64,96},{96,128},{128,160},{160,192},{192,224},{224... | collective-permute-start | bytes 1572872 | tf_op jit(solution)/shard_map/ppermute | solution.py:147
  74.9 13.4 %collective-permute-start.5 = (bf16[128,2048]{1,0:T(8,128)(2,1)}, bf16[128,2048]{1,0:T(8,128)(2,1)}, u32[]{:S(2)}, u32[]{:S(2)}) collective-permute-start(bf16[128,2048]{1,0:T(8,128)(2,1)} %collective-permute-done.3), channel_id=1, source_target_pairs={{0,224},{32,0},{64,32},{96,64},{128,96},{160,128},{192,160},{224,1... | collective-permute-start | bytes 1572872 | tf_op jit(solution)/shard_map/ppermute | solution.py:152
  87.1 12.5 %collective-permute-start.6 = (bf16[128,2048]{1,0:T(8,128)(2,1)S(1)}, bf16[128,2048]{1,0:T(8,128)(2,1)}, u32[]{:S(2)}, u32[]{:S(2)}) collective-permute-start(bf16[128,2048]{1,0:T(8,128)(2,1)S(1)} %collective-permute-done.4), channel_id=1, source_target_pairs={{0,32},{32,64},{64,96},{96,128},{128,160},{160,192},{192,224},{224... | collective-permute-start | bytes 1572872 | tf_op jit(solution)/shard_map/ppermute | solution.py:147
  109.2 41.5 %copy-start.10 = (pred[128,1024]{1,0:T(8,128)(4,1)S(1)}, pred[128,1024]{1,0:T(8,128)(4,1)}, u32[]{:S(2)}) copy-start(pred[128,1024]{1,0:T(8,128)(4,1)} %compare_and_fusion) | copy-start | bytes 393220
  178.0 4.9 copy-start.3
  178.0 239.6 %all-reduce.8.cloned.1.call-start = ((), (), s32[]{:S(2)}) async-start(), calls=%async_computation.3 | async-start | bytes 3670016
  182.7 7.1 %copy-start.14 = (f32[4,8,2]{2,1,0:T(8,128)S(1)}, f32[4,8,2]{2,1,0:T(8,128)}, u32[]{:S(2)}) copy-start(f32[4,8,2]{2,1,0:T(8,128)} %get-tuple-element.28) | copy-start | bytes 772
  182.7 7.2 %copy-start.13 = (f32[128,8,2]{0,2,1:T(2,128)S(1)}, f32[128,8,2]{0,2,1:T(2,128)}, u32[]{:S(2)}) copy-start(f32[128,8,2]{0,2,1:T(2,128)} %get-tuple-element.26) | copy-start | bytes 24580
  182.7 115.4 %copy-start.17 = (s32[128]{0:T(128)S(1)}, s32[128]{0:T(128)}, u32[]{:S(2)}) copy-start(s32[128]{0:T(128)} %and_select_fusion) | copy-start | bytes 1540
  185.7 113.6 %copy-start.6 = (bf16[128,3584]{1,0:T(8,128)(2,1)S(1)}, bf16[128,3584]{1,0:T(8,128)(2,1)}, u32[]{:S(2)}) copy-start(bf16[128,3584]{1,0:T(8,128)(2,1)} %param.17) | copy-start | bytes 2752516
  185.7 115.3 %copy-start.16 = (u32[256]{0:T(256)S(1)}, u32[256]{0:T(256)}, u32[]{:S(2)}) copy-start(u32[256]{0:T(256)} %constant.151) | copy-start | bytes 3076
  185.7 232.9 %copy-start.9 = (bf16[4,3584]{1,0:T(4,128)(2,1)S(1)}, bf16[4,3584]{1,0:T(4,128)(2,1)}, u32[]{:S(2)}) copy-start(bf16[4,3584]{1,0:T(4,128)(2,1)} %param.14) | copy-start | bytes 86020
  185.7 232.9 %copy-start.12 = (f32[3584]{0:T(1024)S(1)}, f32[3584]{0:T(1024)}, u32[]{:S(2)}) copy-start(f32[3584]{0:T(1024)} %get-tuple-element.6) | copy-start | bytes 43012
  185.8 234.0 %copy-start.11 = (f32[3584]{0:T(1024)S(1)}, f32[3584]{0:T(1024)}, u32[]{:S(2)}) copy-start(f32[3584]{0:T(1024)} %get-tuple-element.5) | copy-start | bytes 43012
  300.9 265.7 %all-reduce.10.cloned.1.call-start = ((), (), s32[]{:S(2)}) async-start(), calls=%async_computation.4 | async-start | bytes 1835008
  (7 other events, 19.7 us)
Sparse Core Ops, SparseCore 0:
  40.8 50.2 all-gather.4
  92.8 57.8 all-gather.6
  178.1 119.9 all-reduce.5
  301.3 116.2 all-reduce.7
  454.0 112.5 all-reduce.9
